TPU v7x, 32 devices: a whole 2x2x4 slice. The times are simulated.
32 devices in a mesh: band: 4 (over x, core), freq: 8 (over z, y).
Axes of the slice: x: 2, y: 2, z: 4, core: 2. Of those that a mesh axis runs over, the one named last changes fastest.
Arguments:
- spectrum: float32 [8, 36, 64, 64], P('freq', None, 'band'), may hold values from 0.05 to 1
- velocity: float32 [2, 24, 64, 64], P(None, None, 'band', 'freq'), may hold values from -3 to 3
- gain_matrix: bfloat16 [288, 288], replicated, may hold values from -0.375 to 0.375
- quad_matrix: bfloat16 [288, 288], replicated, may hold values from -0.375 to 0.375
- limiter_flags: int32 [8, 64, 64], replicated, may hold values 0 or 1
- sea_mask: int32 [64, 64], replicated, may hold values 0 or 1
- current_route: int32 [8], replicated, may hold values from 0 to 23
- stokes_route: int32 [8, 4], replicated, may hold values from 0 to 23
Outputs:
- spectrum_out: float32 [8, 36, 64, 64], P('freq', None, 'band')
- velocity_out: float32 [2, 24, 64, 64], P(None, None, 'band', 'freq')
All inputs are finite; a program needn't handle non-finite values.
Results may differ from a plain program's by a relative error of at most 0.00045.
Values sent between devices are 32-bit elements; how exact they have to be, the bound alone decides.
A program may use at most 64 MiB of HBM per device.

v0:
```python
import functools

import jax
import jax.numpy as jnp
import numpy as np
from jax import lax
from jax.experimental import pallas as pl
from jax.experimental.pallas import tpu as pltpu
from jax.sharding import PartitionSpec as P

DIR = 36
LAYERS = 24
SUB = 4
CYCLES = 2
OSTEPS = 3


precise = lax.Precision.HIGHEST
ocean_dt = 0.2
viscous = 0.5
coriolis = 1.0
mixing = 0.5
friction = 0.1


GROUP = 8
LANES = 128
DIRP = -(-DIR // GROUP) * GROUP
GROUPS = DIRP // GROUP
HALO = SUB
DEPTH = CYCLES * SUB
PARTS = ((0, 2), (2, GROUPS))
MESH = pl.DeviceIdType.MESH


def swap_pieces(blocks, piece, width):
    lane = lax.broadcasted_iota(jnp.int32, blocks[0].shape, 1)
    out = list(blocks)
    far = width // 2
    while far:
        low = (lane & (far * piece)) == 0
        for a in range(width):
            if a & far:
                continue
            b = a + far
            x, y = out[a], out[b]
            out[a] = jnp.where(low, x, pltpu.roll(y, far * piece, 1))
            out[b] = jnp.where(low, pltpu.roll(x, LANES - far * piece, 1), y)
        far //= 2
    return out


def packing(rows, planes, pitch, tile_cols):
    places = LANES // tile_cols
    free = set(range(places))
    left = {
        m: [q for q in range(LANES // pitch) if 0 <= m + planes * q - HALO < rows]
        for m in range(planes)
    }
    moves, where = [], {}
    while any(left.values()):
        best = None
        for m in range(planes):
            for by in range(places):
                fits = [
                    q for q in left[m] if (q * pitch // tile_cols + by) % places in free
                ]
                if best is None or len(fits) > len(best[2]):
                    best = (m, by, fits)
        m, by, fits = best
        spots = [(q * pitch // tile_cols + by) % places for q in fits]
        moves.append((m, (by * tile_cols - HALO) % LANES, spots))
        for q, spot in zip(fits, spots):
            where[m + planes * q - HALO] = spot
            free.remove(spot)
            left[m].remove(q)
    return moves, where


def pack(blocks, moves, tile_cols):
    lane = lax.broadcasted_iota(jnp.int32, blocks[0].shape, 1)
    total = None
    for m, shift, spots in moves:
        piece = pltpu.roll(blocks[m], shift, 1) if shift else blocks[m]
        if total is None:
            total = piece
            continue
        hit = None
        for spot in spots:
            one = (lane >= spot * tile_cols) & (lane < (spot + 1) * tile_cols)
            hit = one if hit is None else hit | one
        total = jnp.where(hit, piece, total)
    return total


def parts_of(courant):
    up, down = jnp.maximum(courant, 0.0), jnp.minimum(courant, 0.0)
    return up, down, 0.5 * (courant * courant - (up - down))


def kernel(
    bands,
    freqs,
    cols,
    route,
    stokes_route,
    spectrum,
    velocity,
    gain_in,
    quad_in,
    flags_in,
    sea_in,
    widen_in,
    wave_in,
    trig_in,
    result,
    ocean_out,
    spec,
    halo_low,
    halo_high,
    vel,
    gain_raw,
    quad_raw,
    widen,
    wave,
    trig,
    gain,
    quad,
    flag_raw,
    sea_raw,
    flag_blk,
    sea_blk,
    flag_north,
    flag_east,
    flag_north2,
    flag_east2,
    sea2,
    tile,
    tiles,
    route_out,
    route_own,
    route_low,
    route_high,
    drift,
    faces,
    faces2,
    coef,
    coef2,
    leave,
    arrive,
    first,
    packed,
    back,
    final,
    done,
    ocean,
    weight,
    vout,
    load_sems,
    halo_sems,
    route_sems,
    tile_sems,
    out_sems,
    back_sems,
    store_sems,
):
    band = lax.axis_index("band")
    me = lax.axis_index("freq")
    f32 = jnp.float32
    rows = spectrum.shape[1]
    tile_cols = velocity.shape[2]
    tall = rows + 2 * DEPTH
    block = max(LANES, cols)
    slots = block // cols
    n = tall // slots
    pitch = tile_cols + 2 * HALO
    per = LANES // pitch
    planes = (rows + 2 * HALO) // per
    seam = LANES - pitch
    moves, spot_of = packing(rows, planes, pitch, tile_cols)
    has_low = band > 0
    has_high = band < bands - 1

    def others(fn):
        def step(i, carry):
            fn(lax.rem(me + i, freqs))
            return carry

        lax.fori_loop(1, freqs, step, 0)

    def every(fn):
        def step(i, carry):
            fn(i)
            return carry

        lax.fori_loop(0, freqs, step, 0)

    def copy(src, dst, sems, slot_send, slot_recv, to_band, to_freq):
        return pltpu.make_async_remote_copy(
            src_ref=src,
            dst_ref=dst,
            send_sem=sems.at[(0,) + slot_send],
            recv_sem=sems.at[(1,) + slot_recv],
            device_id=(to_band, to_freq),
            device_id_type=MESH,
        )

    def rolled(x, shift):
        shift %= x.shape[1]
        return pltpu.roll(x, shift, 1) if shift else x

    def strided(ref, size, base, at):
        depth = ref.shape[1]
        if cols > LANES:
            return ref[pl.ds(base, size), at, :]
        return ref.reshape(ref.shape[0] * depth, cols)[
            pl.ds(base * depth + at, size, stride=depth), :
        ]

    def await_bytes(ref, sem):
        pltpu.make_async_copy(ref, ref, sem).wait()

    rest = pl.ds(0, freqs - 1)

    barrier = pltpu.get_barrier_semaphore()

    def greet(to_band, to_freq):
        pl.semaphore_signal(barrier, inc=1, device_id=(to_band, to_freq), device_id_type=MESH)

    load_vel = pltpu.make_async_copy(velocity, vel, load_sems.at[0])
    load_vel.start()
    others(lambda f: greet(band, f))

    @pl.when(has_low)
    def _():
        every(lambda f: greet(band - 1, f))

    @pl.when(has_high)
    def _():
        every(lambda f: greet(band + 1, f))

    load_spec = pltpu.make_async_copy(spectrum, spec.at[pl.ds(0, DIR)], load_sems.at[1])
    load_grid = [
        pltpu.make_async_copy(src, dst, load_sems.at[2 + i])
        for i, (src, dst) in enumerate(((flags_in, flag_raw), (sea_in, sea_raw)))
    ]
    loads = [
        pltpu.make_async_copy(src, dst, load_sems.at[4 + i])
        for i, (src, dst) in enumerate(
            (
                (wave_in, wave),
                (gain_in, gain_raw),
                (quad_in, quad_raw),
                (widen_in, widen),
                (trig_in, trig),
            )
        )
    ]
    for one in load_grid:
        one.start()
    load_spec.start()
    for one in loads:
        one.start()

    load_vel.wait()
    for c in range(2):
        field = vel[c].reshape(rows * tile_cols, LAYERS)
        tile[c * LAYERS : (c + 1) * LAYERS, :] = field.T

    def prepare(f):
        route_out[f, 0:1, :] = tile[pl.ds(route[f], 1), :]
        route_out[f, 1:2, :] = tile[pl.ds(LAYERS + route[f], 1), :]

    every(prepare)
    count = freqs - 1 + freqs * (has_low.astype(jnp.int32) + has_high.astype(jnp.int32))
    pl.semaphore_wait(barrier, count)

    halo_to_low = copy(
        spectrum.at[:, pl.ds(0, DEPTH)], halo_high.at[pl.ds(0, DIR)], halo_sems,
        (0,), (0,), band - 1, me,
    )
    halo_to_high = copy(
        spectrum.at[:, pl.ds(rows - DEPTH, DEPTH)], halo_low.at[pl.ds(0, DIR)], halo_sems,
        (1,), (1,), band + 1, me,
    )

    def route_copy(f):
        return copy(route_out.at[f], route_own.at[me], route_sems, (0,), (0,), band, f)

    def route_to_low(f):
        return copy(
            route_out.at[f], route_high.at[me], route_sems, (1,), (1,), band - 1, f
        )

    def route_to_high(f):
        return copy(
            route_out.at[f], route_low.at[me], route_sems, (2,), (2,), band + 1, f
        )

    others(lambda f: route_copy(f).start())

    @pl.when(has_low)
    def _():
        every(lambda f: route_to_low(f).start())
        halo_to_low.start()

    @pl.when(has_high)
    def _():
        every(lambda f: route_to_high(f).start())
        halo_to_high.start()

    def near_tiles(fn):
        for down in (-1, 0, 1):
            for side in (-1, 0, 1):
                if down == 0 and side == 0:
                    continue
                to_band, to_freq = band + down, me + side
                there = (to_band >= 0) & (to_band < bands) & (to_freq >= 0) & (to_freq < freqs)
                mine = 3 * (1 + down) + 1 + side
                fn(there, mine, 8 - mine, to_band, to_freq)

    def tile_copy(mine, theirs, to_band, to_freq):
        return copy(tile, tiles.at[theirs], tile_sems, (), (), to_band, to_freq)

    def tile_start(there, mine, theirs, to_band, to_freq):
        @pl.when(there)
        def _():
            tile_copy(mine, theirs, to_band, to_freq).start()

        @pl.when(jnp.logical_not(there))
        def _():
            tiles[mine] = jnp.zeros_like(tile)

    near_tiles(tile_start)
    tiles[4] = tile[...]
    route_own[me] = route_out[me]

    pads = ((DIR, DIRP - DIR),)
    for at, size in pads:
        spec[at : at + size] = jnp.zeros((size, rows, cols), f32)
        halo_low[at : at + size] = jnp.zeros((size, DEPTH, cols), f32)
        halo_high[at : at + size] = jnp.zeros((size, DEPTH, cols), f32)

    @pl.when(jnp.logical_not(has_low))
    def _():
        halo_low[...] = jnp.zeros_like(halo_low)
        route_low[...] = jnp.zeros_like(route_low)

    @pl.when(jnp.logical_not(has_high))
    def _():
        halo_high[...] = jnp.zeros_like(halo_high)
        route_high[...] = jnp.zeros_like(route_high)

    for one in load_grid:
        one.wait()

    steps = CYCLES * SUB
    all_rows = sea_raw.shape[0]
    wide = (8, block)

    def grid_row(at):
        whole = jnp.clip(band * rows - DEPTH + at, 0, all_rows - 1)
        there = has_low if at < DEPTH else (None if at < DEPTH + rows else has_high)
        flag = strided(flag_raw, steps, 0, whole)
        sea = sea_raw[pl.ds(whole, 1), :].astype(f32)
        flag = flag.astype(f32)
        if there is not None:
            there = there.astype(f32)
            flag, sea = flag * there, sea * there
        return flag, sea

    for k in range(n):
        pieces = [grid_row(k + n * s) for s in range(slots)]
        flag_blk[k] = jnp.concatenate([flag for flag, _ in pieces], axis=1)
        sea = jnp.concatenate([sea for _, sea in pieces], axis=1)
        sea_blk[8 * k : 8 * (k + 1), :] = jnp.broadcast_to(sea, wide)

    for k in range(n):
        here = flag_blk[k]
        above = flag_blk[k + 1] if k + 1 < n else rolled(flag_blk[0], -cols)
        beside = rolled(here, -1)
        for sub in range(SUB):
            there = slice(8 * k, 8 * (k + 1))
            flag_north[sub, there, :] = jnp.broadcast_to(above[sub : sub + 1], wide)
            flag_east[sub, there, :] = jnp.broadcast_to(beside[sub : sub + 1], wide)

    lane = lax.broadcasted_iota(jnp.int32, (8, LANES), 1)
    column = me * tile_cols - HALO + (lane & (pitch - 1))
    inside = (column >= 0) & (column < cols)
    window_flags, window_sea = [], []
    for m in range(planes):
        total_flags, total_sea = jnp.zeros((8, LANES), f32), jnp.zeros((8, LANES), f32)
        for q in range(per):
            at = m + planes * q + DEPTH - HALO
            k, s = at % n, at // n
            shift = lax.rem(q * pitch - cols * s - tile_cols * me + HALO + 2 * block, block)
            hit = (lane >= q * pitch) & (lane < (q + 1) * pitch) & inside
            total_flags = jnp.where(
                hit, pltpu.roll(flag_blk[k], shift, 1)[:, :LANES], total_flags
            )
            total_sea = jnp.where(hit, pltpu.roll(sea_blk[8 * k : 8 * (k + 1), :], shift, 1)[:, :LANES], total_sea)
        window_flags.append(total_flags)
        window_sea.append(total_sea)
    for m in range(planes):
        sea2[m] = jnp.concatenate([window_sea[m]] * GROUPS, axis=0)
        above = window_flags[m + 1] if m + 1 < planes else rolled(window_flags[0], -pitch)
        beside = rolled(window_flags[m], -1)
        for sub in range(SUB):
            step = SUB + sub
            flag_north2[sub, m] = jnp.broadcast_to(above[step : step + 1], (DIRP, LANES))
            flag_east2[sub, m] = jnp.broadcast_to(beside[step : step + 1], (DIRP, LANES))

    load_spec.wait()
    for one in loads:
        one.wait()

    for raw, padded in ((gain_raw, gain), (quad_raw, quad)):
        half = jnp.dot(widen[...], raw[...], preferred_element_type=f32).astype(jnp.bfloat16)
        padded[...] = lax.dot_general(
            half, widen[...], (((1,), (1,)), ((), ())), preferred_element_type=f32
        ).astype(jnp.bfloat16)

    layer = lax.broadcasted_iota(jnp.int32, (LAYERS, 1), 0)
    component = lax.broadcasted_iota(jnp.int32, (LAYERS, freqs * DIRP), 1)
    deposits = jnp.zeros((LAYERS, freqs * DIRP), f32)
    for g in range(freqs):
        deposit = jnp.zeros((LAYERS, 1), f32)
        for j in range(stokes_route.shape[0]):
            hit = (layer == stokes_route[j, g]).astype(f32)
            deposit = deposit + hit * (1.0 / (1.0 + j))
        own = (component >= g * DIRP) & (component < (g + 1) * DIRP)
        deposits = jnp.where(own, deposit, deposits)
    for c in range(2):
        weight[c * LAYERS : (c + 1) * LAYERS, :] = deposits * trig[c : c + 1, :]

    await_bytes(route_own.at[rest], route_sems.at[1, 0])

    @pl.when(has_low)
    def _():
        await_bytes(route_low, route_sems.at[1, 2])

    @pl.when(has_high)
    def _():
        await_bytes(route_high, route_sems.at[1, 1])

    stacks = [
        jnp.concatenate(
            [route_low[j], route_own[j], route_high[j], jnp.zeros((2, LANES), f32)], axis=0
        )
        for j in range(freqs)
    ]
    across = []
    for row in range(rows):
        halves = []
        for half in range(block // LANES):
            total = jnp.zeros((8, LANES), f32)
            reach = min(cols, LANES) // tile_cols
            turned = [
                rolled(stacks[half * reach + j], (j - row) * tile_cols) for j in range(reach)
            ]
            for j, one in enumerate(turned):
                lead = j * tile_cols
                total = jnp.where((lane >= lead) & (lane < lead + tile_cols), one, total)
            halves.append(total)
        across.append(jnp.concatenate(halves, axis=1))
    spreads = 0.15 * jnp.tanh(jnp.concatenate(across, axis=0))
    moved = [spreads] + [rolled(spreads, cols * s) for s in range(1, slots)]
    for row in range(rows):
        for source in range(3):
            at = row + DEPTH + rows * (source - 1)
            if at < 0 or at >= tall:
                continue
            k, s = at % n, at // n
            for c in range(2):
                line = 8 * row + 2 * source + c
                drift[c, k : k + 1, cols * s : cols * (s + 1)] = moved[s][
                    line : line + 1, cols * s : cols * (s + 1)
                ]
    blane = lax.broadcasted_iota(jnp.int32, (1, block), 1)
    last = ((blane & (cols - 1)) == cols - 1).astype(f32)
    inner = 1.0 - last
    east, north = drift[0], drift[1]
    above = jnp.concatenate([north[1:], rolled(north[0:1], -cols)], axis=0)
    for i, face in enumerate(
        (0.5 * (north + above), 0.5 * (inner * east + rolled(east, -1)), 0.5 * east)
    ):
        for k in range(n):
            faces[i, 8 * k : 8 * (k + 1), :] = jnp.broadcast_to(face[k : k + 1], wide)

    @pl.when(has_low)
    def _():
        halo_to_high.wait_recv()

    @pl.when(has_high)
    def _():
        halo_to_low.wait_recv()

    number = me.astype(f32) + 0.5
    my_rate = 0.5 + 0.3 * number / freqs

    def row_of(base, at):
        if at < DEPTH:
            return strided(halo_low, GROUP, base, at)
        if at < DEPTH + rows:
            return strided(spec, GROUP, base, at - DEPTH)
        return strided(halo_high, GROUP, base, at - DEPTH - rows)

    def up(x, by):
        return jnp.concatenate([x[8:], rolled(x[:8], -by)], axis=0)

    def down(x, by):
        return jnp.concatenate([rolled(x[-8:], by), x[:-8]], axis=0)

    def advect_first(group, carry):
        base = pl.multiple_of(group * GROUP, GROUP)
        table = wave[pl.ds(base, GROUP), :]

        def rate_of(i):
            rate = jnp.broadcast_to(table[:, i : i + 1] * my_rate, wide)
            return jnp.concatenate([rate] * n, axis=0)

        rate_east = rate_of(0)
        for axis, rate in ((0, rate_of(1)), (1, rate_east)):
            for i, one in enumerate(parts_of(rate + faces[axis])):
                coef[3 * axis + i] = one
        coef[6] = 1.0 - last * jnp.maximum(rate_east + faces[2], 0.0)
        state = jnp.concatenate(
            [
                jnp.concatenate([row_of(base, k + n * s) for s in range(slots)], axis=1)
                for k in range(n)
            ],
            axis=0,
        )
        for sub in range(SUB):
            more = flag_north[sub] * coef[2]
            flux = (coef[0] + more) * state + (coef[1] - more) * up(state, cols)
            state = state - (flux - down(flux, cols))
            more = flag_east[sub] * coef[5]
            flux = (coef[3] + more) * (inner * state) + (coef[4] - more) * rolled(state, -1)
            state = (coef[6] * state - (inner * flux - rolled(flux, 1))) * sea_blk[...]
        width = min(cols, LANES) // pitch
        low_half = lax.broadcasted_iota(jnp.int32, (8 * planes, LANES), 1) < width * pitch
        for odd in range(2):
            turned = rolled(state, HALO - odd * tile_cols)
            for half in range(block // LANES):
                sources = []
                for i in range(width):
                    pieces = []
                    for s in range(slots):
                        lines = []
                        for m in range(planes):
                            at = m + planes * (i + width * s) + DEPTH - HALO
                            assert at // n == s
                            k = at % n
                            lines.append(
                                turned[8 * k : 8 * (k + 1), half * LANES : (half + 1) * LANES]
                            )
                        pieces.append(jnp.concatenate(lines, axis=0))
                    sources.append(pieces[0] if slots == 1 else jnp.where(low_half, *pieces))
                for e, one in enumerate(swap_pieces(sources, pitch, width)):
                    to = 2 * (e + width * half) + odd
                    for m in range(planes):
                        leave[to, pl.ds(base, GROUP), m * LANES : (m + 1) * LANES] = one[
                            8 * m : 8 * (m + 1)
                        ]
        return carry

    def part_rows(part):
        low, high = PARTS[part]
        return pl.ds(low * GROUP, (high - low) * GROUP)

    def out_copy(part, f):
        there = part_rows(part)
        return copy(
            leave.at[f, there], arrive.at[me, there], out_sems, (part,), (part,), band, f
        )

    for part, (low, high) in enumerate(PARTS):
        lax.fori_loop(low, high, advect_first, 0)
        others(lambda f: out_copy(part, f).start())
    arrive[me] = leave[me]

    deep = 1 + has_low.astype(jnp.int32) + has_high.astype(jnp.int32)
    broad = 1 + (me > 0).astype(jnp.int32) + (me < freqs - 1).astype(jnp.int32)

    def await_tiles(way):
        for a in (2, 3):
            for b in (2, 3):

                @pl.when((deep == a) & (broad == b))
                def _():
                    await_bytes(tiles.at[pl.ds(0, a * b - 1)], tile_sems.at[way])

    await_tiles(1)
    tall_lane = lax.broadcasted_iota(jnp.int32, tile.shape, 1)
    for m in range(planes):
        total = jnp.zeros(tile.shape, f32)
        for q in range(per):
            row = m + planes * q - HALO
            down = 0 if row < 0 else (1 if row < rows else 2)
            from_row = row + rows * (1 - down)
            lead = q * pitch
            for side, width, from_col in (
                (0, HALO, tile_cols - HALO), (1, tile_cols, 0), (2, HALO, 0),
            ):
                piece = rolled(tiles[3 * down + side], lead - from_row * tile_cols - from_col)
                total = jnp.where((tall_lane >= lead) & (tall_lane < lead + width), piece, total)
                lead += width
        ocean[:, m * LANES : (m + 1) * LANES] = total

    def face_step(g, carry):
        east = 0.15 * jnp.tanh(ocean[pl.ds(route[g], 1), :])
        north = 0.15 * jnp.tanh(ocean[pl.ds(LAYERS + route[g], 1), :])
        for m in range(planes):
            here = north[:, m * LANES : (m + 1) * LANES]
            above = (
                north[:, (m + 1) * LANES : (m + 2) * LANES]
                if m + 1 < planes
                else rolled(north[:, :LANES], -pitch)
            )
            faces2[g, m : m + 1, :] = 0.5 * (here + above)
            here = east[:, m * LANES : (m + 1) * LANES]
            faces2[g, planes + m : planes + m + 1, :] = 0.5 * (here + rolled(here, -1))
        return carry

    lax.fori_loop(0, freqs, face_step, 0)

    for part in range(len(PARTS)):
        await_bytes(arrive.at[rest, part_rows(part)], out_sems.at[1, part])

    def source(whole):
        grown = jnp.dot(gain[...], whole.astype(jnp.bfloat16), preferred_element_type=f32)
        quartic = jnp.dot(
            quad[...], (whole * whole).astype(jnp.bfloat16), preferred_element_type=f32
        )
        return whole * (1.0 + 0.5 * jnp.tanh(grown) - 0.25 * jnp.tanh(quartic))

    total_rows = freqs * DIRP
    for m in range(planes):
        there = slice(m * LANES, (m + 1) * LANES)
        whole = arrive[:, :, there].reshape(total_rows, LANES) * sea2[m][0:1]
        first[:, :, there] = source(whole).reshape(freqs, DIRP, LANES)

    def advect_second(g, carry):
        rate = 0.5 + 0.3 * (g.astype(f32) + 0.5) / freqs
        table = wave[...] * rate
        rate_east = jnp.broadcast_to(table[:, 0:1], (DIRP, LANES))
        rate_north = jnp.broadcast_to(table[:, 1:2], (DIRP, LANES))
        state = [first[g, :, m * LANES : (m + 1) * LANES] for m in range(planes)]
        for m in range(planes):
            for axis, rate in ((0, rate_north), (planes, rate_east)):
                face = faces2[g, axis + m : axis + m + 1, :]
                for i, one in enumerate(parts_of(rate + face)):
                    coef2[3 * (axis + m) + i] = one
        for sub in range(SUB):
            fluxes = []
            for m in range(planes):
                here = 3 * m
                more = flag_north2[sub, m] * coef2[here + 2]
                above = state[m + 1] if m + 1 < planes else rolled(state[0], -pitch)
                fluxes.append(
                    (coef2[here] + more) * state[m] + (coef2[here + 1] - more) * above
                )
            cells = [
                state[m] - (fluxes[m] - (fluxes[m - 1] if m else rolled(fluxes[-1], pitch)))
                for m in range(planes)
            ]
            fluxes = []
            for m in range(planes):
                here = 3 * (planes + m)
                more = flag_east2[sub, m] * coef2[here + 2]
                fluxes.append(
                    (coef2[here] + more) * cells[m]
                    + (coef2[here + 1] - more) * rolled(cells[m], -1)
                )
            state = [
                (cells[m] - (fluxes[m] - rolled(fluxes[m], 1))) * sea2[m] for m in range(planes)
            ]
        packed[g] = pack(state, moves, tile_cols)
        return carry

    lax.fori_loop(0, freqs, advect_second, 0)
    back[...] = source(packed[...].reshape(total_rows, LANES)).reshape(freqs, DIRP, LANES)

    def back_copy(f):
        return copy(back.at[f], final.at[me], back_sems, (), (), band, f)

    others(lambda f: back_copy(f).start())
    final[me] = back[me]

    stokes = jnp.dot(
        weight[...], arrive[...].reshape(total_rows, planes * LANES),
        precision=precise, preferred_element_type=f32,
    )
    level = lax.broadcasted_iota(jnp.int32, (LAYERS, LANES), 0)
    planes_of = range(planes)

    def split(x, c):
        return [
            x[c * LAYERS : (c + 1) * LAYERS, m * LANES : (m + 1) * LANES] for m in planes_of
        ]

    def spreading(field):
        outs = []
        for m in planes_of:
            here = field[m]
            above = field[m + 1] if m + 1 < planes else rolled(field[0], -pitch)
            below = field[m - 1] if m else rolled(field[-1], pitch)
            sides = rolled(here, 1) + rolled(here, -1)
            over = jnp.where(level < LAYERS - 1, pltpu.roll(here, LAYERS - 1, 0), 0.0)
            under = jnp.where(level > 0, pltpu.roll(here, 1, 0), 0.0)
            outs.append(
                viscous * (sides + above + below - 4.0 * here)
                + mixing * (over + under - 2.0 * here)
                - friction * here
            )
        return outs

    both = ocean[...]
    u, v = split(both, 0), split(both, 1)
    stokes_east, stokes_north = split(stokes, 0), split(stokes, 1)
    for _ in range(OSTEPS):
        change_u, change_v = spreading(u), spreading(v)
        u, v = (
            [
                (u[m] + ocean_dt * (change_u[m] + coriolis * (v[m] + stokes_north[m])))
                * sea2[m][0:1]
                for m in planes_of
            ],
            [
                (v[m] + ocean_dt * (change_v[m] - coriolis * (u[m] + stokes_east[m])))
                * sea2[m][0:1]
                for m in planes_of
            ],
        )
    for c, field in enumerate((u, v)):
        turned = pack(field, moves, tile_cols).T
        for row in range(rows):
            spot = spot_of[row]
            vout[c, row] = turned[spot * tile_cols : (spot + 1) * tile_cols, :]
    store_ocean = pltpu.make_async_copy(vout, ocean_out, store_sems.at[1])
    store_ocean.start()

    await_bytes(route_out.at[rest], route_sems.at[0, 0])

    @pl.when(has_low)
    def _():
        await_bytes(route_out, route_sems.at[0, 1])
        halo_to_low.wait_send()

    @pl.when(has_high)
    def _():
        await_bytes(route_out, route_sems.at[0, 2])
        halo_to_high.wait_send()

    await_tiles(0)
    for part in range(len(PARTS)):
        await_bytes(leave.at[rest, part_rows(part)], out_sems.at[0, part])

    await_bytes(final.at[rest], back_sems.at[1])
    width = min(freqs, LANES // tile_cols)
    reach = width * tile_cols
    row_at = {spot: row for row, spot in spot_of.items()}
    for chunk in range(freqs // width):
        columns = [final[chunk * width + j] for j in range(width)]
        for i, one in enumerate(swap_pieces(columns, tile_cols, width)):
            for s in range(LANES // reach):
                row = row_at[s * width + i]
                cells = rolled(one, -s * reach)[:, :reach]
                if cols > LANES:
                    done[:, row, chunk * reach : (chunk + 1) * reach] = cells
                else:
                    done.reshape(DIRP * rows, cols)[pl.ds(row, DIRP, stride=rows), :] = cells
    store = pltpu.make_async_copy(done.at[pl.ds(0, DIR)], result, store_sems.at[0])
    store.start()
    await_bytes(back.at[rest], back_sems.at[0])
    store_ocean.wait()
    store.wait()


def body(
    spectrum,
    velocity,
    gain_matrix,
    quad_matrix,
    limiter_flags,
    sea_mask,
    current_route,
    stokes_route,
):
    bands = lax.axis_size("band")
    freqs = lax.axis_size("freq")
    rows, cols = spectrum.shape[2:]
    tile_cols = velocity.shape[3]
    pitch = tile_cols + 2 * HALO
    planes = (rows + 2 * HALO) * pitch // LANES
    tall = rows + 2 * DEPTH
    block = max(LANES, cols)
    n = tall * cols // block
    parts = freqs * DIRP
    assert CYCLES == 2 and spectrum.shape[0] == 1 and rows % 8 == 0 and DEPTH % 8 == 0
    assert rows * tile_cols == LANES and rows >= DEPTH and tile_cols >= HALO >= OSTEPS
    assert pitch == 2 * tile_cols and LANES % pitch == 0 and freqs * tile_cols == cols
    assert (rows + 2 * HALO) % (LANES // pitch) == 0 and cols & (cols - 1) == 0
    assert block % cols == 0 and n * block == tall * cols and cols % pitch == 0
    assert bands > 1 and freqs > 1 and CYCLES * SUB == 8 and 2 * planes <= 8 and block // cols <= 2
    angles = (np.arange(DIR) + 0.5) * (2.0 * np.pi / DIR)
    waves = np.stack([np.cos(angles), np.sin(angles)])
    wave = np.zeros((DIRP, 2), np.float32)
    wave[:DIR] = waves.T
    factor = (0.5 + 1.5 * (np.arange(freqs) + 0.5) / freqs) * DIR ** (-0.5)
    trig = np.zeros((2, freqs, DIRP), np.float32)
    trig[:, :, :DIR] = waves[:, None, :] * factor[None, :, None]
    comps = freqs * DIR
    widen = np.zeros((parts, comps), np.float32)
    index = np.arange(comps)
    widen[index // DIR * DIRP + index % DIR, index] = 1.0
    f32, bf16 = jnp.float32, jnp.bfloat16
    anywhere = pl.BlockSpec(memory_space=pl.ANY)
    scalars = pl.BlockSpec(memory_space=pltpu.SMEM)
    dma = pltpu.SemaphoreType.DMA
    vmem = pltpu.VMEM
    tile_cells = rows * tile_cols
    layers = 2 * LAYERS
    result, ocean = pl.pallas_call(
        functools.partial(kernel, bands, freqs, cols),
        out_shape=(
            jax.ShapeDtypeStruct((DIR, rows, cols), f32),
            jax.ShapeDtypeStruct((2, rows, tile_cols, LAYERS), f32),
        ),
        in_specs=[scalars] * 2 + [anywhere] * 9,
        out_specs=(anywhere, anywhere),
        scratch_shapes=[
            vmem((DIRP, rows, cols), f32),
            vmem((DIRP, DEPTH, cols), f32),
            vmem((DIRP, DEPTH, cols), f32),
            vmem((2, rows, tile_cols, LAYERS), f32),
            vmem((comps, comps), bf16),
            vmem((comps, comps), bf16),
            vmem((parts, comps), bf16),
            vmem((DIRP, 2), f32),
            vmem((2, parts), f32),
            vmem((parts, parts), bf16),
            vmem((parts, parts), bf16),
            vmem(limiter_flags.shape, jnp.int32),
            vmem(sea_mask.shape, jnp.int32),
            vmem((n, 8, block), f32),
            vmem((8 * n, block), f32),
            vmem((SUB, 8 * n, block), f32),
            vmem((SUB, 8 * n, block), f32),
            vmem((SUB, planes, DIRP, LANES), f32),
            vmem((SUB, planes, DIRP, LANES), f32),
            vmem((planes, DIRP, LANES), f32),
            vmem((layers, tile_cells), f32),
            vmem((9, layers, tile_cells), f32),
            vmem((freqs, 2, tile_cells), f32),
            vmem((freqs, 2, tile_cells), f32),
            vmem((freqs, 2, tile_cells), f32),
            vmem((freqs, 2, tile_cells), f32),
            vmem((2, n, block), f32),
            vmem((3, 8 * n, block), f32),
            vmem((freqs, 8, LANES), f32),
            vmem((7, 8 * n, block), f32),
            vmem((6 * planes, DIRP, LANES), f32),
            vmem((freqs, DIRP, planes * LANES), f32),
            vmem((freqs, DIRP, planes * LANES), f32),
            vmem((freqs, DIRP, planes * LANES), f32),
            vmem((freqs, DIRP, LANES), f32),
            vmem((freqs, DIRP, LANES), f32),
            vmem((freqs, DIRP, LANES), f32),
            vmem((DIRP, rows, cols), f32),
            vmem((layers, planes * LANES), f32),
            vmem((layers, parts), f32),
            vmem((2, rows, tile_cols, LAYERS), f32),
            dma((9,)),
            dma((2, 2)),
            dma((2, 3)),
            dma((2,)),
            dma((2, len(PARTS))),
            dma((2,)),
            dma((2,)),
        ],
        compiler_params=pltpu.CompilerParams(
            collective_id=0, has_side_effects=True, vmem_limit_bytes=60 * 1024 * 1024
        ),
    )(
        current_route,
        stokes_route.T,
        spectrum.reshape(DIR, rows, cols),
        velocity.transpose(0, 2, 3, 1),
        gain_matrix,
        quad_matrix,
        limiter_flags,
        sea_mask,
        jnp.asarray(widen, bf16),
        jnp.asarray(wave),
        jnp.asarray(trig.reshape(2, parts)),
    )
    return (result.reshape(1, DIR, rows, cols), ocean.transpose(0, 3, 1, 2))


def solution(mesh):
    return jax.shard_map(
        body,
        mesh=mesh,
        in_specs=(
            P("freq", None, "band", None),
            P(None, None, "band", "freq"),
            P(),
            P(),
            P(),
            P(),
            P(),
            P(),
        ),
        out_specs=(P("freq", None, "band", None), P(None, None, "band", "freq")),
        check_vma=False,
    )
```

profile of v0, /device:TPU:0, one launch (start us, length us, event | category | flops | bytes accessed | tf_op | source)
XLA Modules:
  0.0 46.4 jit_solution(14745776794920515139)
XLA Ops:
  0.6 43.4 %shard_map.122 = (f32[36,16,64]{2,1,0:T(8,128)}, f32[2,16,8,24]{3,2,1,0:T(8,128)}) custom-call(s32[8]{0:T(128)} %route.1, s32[4,8]{1,0:T(4,128)} %bitcast.9, f32[36,16,64]{2,1,0:T(8,128)} %bitcast.6, f32[2,16,8,24]{3,2,1,0:T(8,128)} %bitcast.7, bf16[288,288]{1,0:T(8,128)(2,1)} %gain_in.1, bf16[288,288]{1,0:T(8,128)(2,1)} %quad_in.1, s32[8,64,64]{2,1,0:T(8,128)} %flags_in.1, ...), custom_call_target="tpu_custom_call" | custom-call | tf_op jit(solution)/shard_map/pallas_call | solution.py:825
  44.0 0.0 copy-start
  44.0 1.7 %copy.15 = f32[1,36,16,64]{3,2,1,0:T(8,128)} copy(f32[1,36,16,64]{3,2,1,0:T(8,128)} %bitcast.5) | data formatting | bytes 294912
  45.8 0.0 copy-done
  45.8 0.7 %copy.16 = f32[2,24,16,8]{1,3,2,0:T(8,128)} copy(f32[2,24,16,8]{1,3,2,0:T(8,128)S(1)} %bitcast.8) | data formatting | bytes 49152
Async XLA Ops:
  44.0 1.7 %copy-start = (f32[2,16,8,24]{3,2,1,0:T(8,128)S(1)}, f32[2,16,8,24]{3,2,1,0:T(8,128)}, u32[]{:S(2)}) copy-start(f32[2,16,8,24]{3,2,1,0:T(8,128)} %get-tuple-element.5) | copy-start | bytes 73732
where the time goes:
time: 46.6 us; the launch traced here: 46.4 us
  Pallas kernels  43.4 us (93%)
  local copies, waits for them, and re-layouts  2.39 us (5%)
  between operations  0.65 us (1%)
    pallas_call x1, Pallas kernels, body(): pl.pallas_call(functools.partial(kernel, bands, freqs, cols), out_shape=(...  43.4 us
    unnamed x4, local copies, waits for them, and re-layouts  2.39 us

commit v1 on v0

--- a/solution.py
+++ b/solution.py
@@ -512,7 +512,7 @@
         return jnp.concatenate([rolled(x[-8:], by), x[:-8]], axis=0)
 
     def advect_first(group, carry):
-        base = pl.multiple_of(group * GROUP, GROUP)
+        base = group * GROUP
         table = wave[pl.ds(base, GROUP), :]
 
         def rate_of(i):
@@ -576,7 +576,7 @@
         )
 
     for part, (low, high) in enumerate(PARTS):
-        lax.fori_loop(low, high, advect_first, 0)
+        [advect_first(i, 0) for i in range(low, high)]
         others(lambda f: out_copy(part, f).start())
     arrive[me] = leave[me]
 
@@ -679,7 +679,7 @@
         packed[g] = pack(state, moves, tile_cols)
         return carry
 
-    lax.fori_loop(0, freqs, advect_second, 0)
+    [advect_second(jnp.int32(g), 0) for g in range(freqs)]
     back[...] = source(packed[...].reshape(total_rows, LANES)).reshape(freqs, DIRP, LANES)
 
     def back_copy(f):

time: 46.6 us -> 37.5 us (0.80)
  Pallas kernels: 43.4 us -> 34.3 us
    pallas_call x1, Pallas kernels: 43.4 us -> 34.3 us  [body(): pl.pallas_call(functools.partial(kernel, bands, freqs, cols), out_shape=(...]
where the time goes in v1:
time: 37.5 us; the launch traced here: 37.3 us
  Pallas kernels  34.3 us (91%)
  local copies, waits for them, and re-layouts  2.39 us (6%)
  between operations  0.65 us (2%)
    pallas_call x1, Pallas kernels, body(): pl.pallas_call(functools.partial(kernel, bands, freqs, cols), out_shape=(...  34.3 us
    unnamed x4, local copies, waits for them, and re-layouts  2.39 us

profile of v1, /device:TPU:0, one launch (start us, length us, event | category | flops | bytes accessed | tf_op | source)
XLA Modules:
  0.0 37.3 jit_solution(5760485801511561779)
XLA Ops:
  0.6 34.3 %shard_map.122 = (f32[36,16,64]{2,1,0:T(8,128)}, f32[2,16,8,24]{3,2,1,0:T(8,128)}) custom-call(s32[8]{0:T(128)} %route.1, s32[4,8]{1,0:T(4,128)} %bitcast.9, f32[36,16,64]{2,1,0:T(8,128)} %bitcast.6, f32[2,16,8,24]{3,2,1,0:T(8,128)} %bitcast.7, bf16[288,288]{1,0:T(8,128)(2,1)} %gain_in.1, bf16[288,288]{1,0:T(8,128)(2,1)} %quad_in.1, s32[8,64,64]{2,1,0:T(8,128)} %flags_in.1, ...), custom_call_target="tpu_custom_call" | custom-call | tf_op jit(solution)/shard_map/pallas_call | solution.py:825
  34.9 0.0 copy-start
  34.9 1.7 %copy.15 = f32[1,36,16,64]{3,2,1,0:T(8,128)} copy(f32[1,36,16,64]{3,2,1,0:T(8,128)} %bitcast.5) | data formatting | bytes 294912
  36.6 0.0 copy-done
  36.7 0.7 %copy.16 = f32[2,24,16,8]{1,3,2,0:T(8,128)} copy(f32[2,24,16,8]{1,3,2,0:T(8,128)S(1)} %bitcast.8) | data formatting | bytes 49152
Async XLA Ops:
  34.9 1.7 %copy-start = (f32[2,16,8,24]{3,2,1,0:T(8,128)S(1)}, f32[2,16,8,24]{3,2,1,0:T(8,128)}, u32[]{:S(2)}) copy-start(f32[2,16,8,24]{3,2,1,0:T(8,128)} %get-tuple-element.5) | copy-start | bytes 73732

commit v2 on v1

--- a/solution.py
+++ b/solution.py
@@ -29,7 +29,7 @@
 GROUPS = DIRP // GROUP
 HALO = SUB
 DEPTH = CYCLES * SUB
-PARTS = ((0, 2), (2, GROUPS))
+PARTS = ((0, 1), (1, 3), (3, GROUPS))
 MESH = pl.DeviceIdType.MESH
 
 
@@ -102,8 +102,8 @@
     bands,
     freqs,
     cols,
-    route,
-    stokes_route,
+    route_in,
+    stokes_in,
     spectrum,
     velocity,
     gain_in,
@@ -113,8 +113,10 @@
     widen_in,
     wave_in,
     trig_in,
-    result,
+    final,
     ocean_out,
+    route,
+    stokes_route,
     spec,
     halo_low,
     halo_high,
@@ -136,6 +138,7 @@
     flag_east2,
     sea2,
     tile,
+    ready,
     tiles,
     route_out,
     route_own,
@@ -151,11 +154,9 @@
     first,
     packed,
     back,
-    final,
-    done,
     ocean,
     weight,
-    vout,
+    flat,
     load_sems,
     halo_sems,
     route_sems,
@@ -181,19 +182,21 @@
     has_low = band > 0
     has_high = band < bands - 1
 
+    mid = freqs // 2
+    side, place = me // mid, lax.rem(me, mid)
+    near = [side * mid + lax.rem(place + i, mid) for i in [*range(2, mid), 1][: mid - 1]]
+    far = [(1 - side) * mid + lax.rem(2 * mid - 1 - place - i, mid) for i in range(mid)]
+    partners = []
+    for i in range(mid):
+        partners += near[i : i + 1] + [far[i]]
+
     def others(fn):
-        def step(i, carry):
-            fn(lax.rem(me + i, freqs))
-            return carry
-
-        lax.fori_loop(1, freqs, step, 0)
+        for f in partners:
+            fn(f)
 
     def every(fn):
-        def step(i, carry):
-            fn(i)
-            return carry
-
-        lax.fori_loop(0, freqs, step, 0)
+        for f in range(freqs):
+            fn(f)
 
     def copy(src, dst, sems, slot_send, slot_recv, to_band, to_freq):
         return pltpu.make_async_remote_copy(
@@ -227,18 +230,22 @@
     def greet(to_band, to_freq):
         pl.semaphore_signal(barrier, inc=1, device_id=(to_band, to_freq), device_id_type=MESH)
 
+    others(lambda f: greet(band, f))
+
+    @pl.when(has_low)
+    def _():
+        every(lambda f: greet(band - 1, f))
+
+    @pl.when(has_high)
+    def _():
+        every(lambda f: greet(band + 1, f))
+
     load_vel = pltpu.make_async_copy(velocity, vel, load_sems.at[0])
     load_vel.start()
-    others(lambda f: greet(band, f))
-
-    @pl.when(has_low)
-    def _():
-        every(lambda f: greet(band - 1, f))
-
-    @pl.when(has_high)
-    def _():
-        every(lambda f: greet(band + 1, f))
-
+    load_route = pltpu.make_async_copy(route_in, route, load_sems.at[9])
+    load_route.start()
+    load_stokes = pltpu.make_async_copy(stokes_in, stokes_route, load_sems.at[10])
+    load_stokes.start()
     load_spec = pltpu.make_async_copy(spectrum, spec.at[pl.ds(0, DIR)], load_sems.at[1])
     load_grid = [
         pltpu.make_async_copy(src, dst, load_sems.at[2 + i])
@@ -267,10 +274,15 @@
         field = vel[c].reshape(rows * tile_cols, LAYERS)
         tile[c * LAYERS : (c + 1) * LAYERS, :] = field.T
 
+    ready[...] = pltpu.roll(
+        0.15 * jnp.tanh(tile[...]), lax.rem(me * tile_cols, LANES), 1
+    )
+
     def prepare(f):
-        route_out[f, 0:1, :] = tile[pl.ds(route[f], 1), :]
-        route_out[f, 1:2, :] = tile[pl.ds(LAYERS + route[f], 1), :]
-
+        route_out[f, 0:1, :] = ready[pl.ds(route[f], 1), :]
+        route_out[f, 1:2, :] = ready[pl.ds(LAYERS + route[f], 1), :]
+
+    load_route.wait()
     every(prepare)
     count = freqs - 1 + freqs * (has_low.astype(jnp.int32) + has_high.astype(jnp.int32))
     pl.semaphore_wait(barrier, count)
@@ -411,6 +423,7 @@
             flag_east2[sub, m] = jnp.broadcast_to(beside[step : step + 1], (DIRP, LANES))
 
     load_spec.wait()
+    load_stokes.wait()
     for one in loads:
         one.wait()
 
@@ -449,30 +462,31 @@
         )
         for j in range(freqs)
     ]
-    across = []
+    reach = min(cols, LANES) // tile_cols
+    places = LANES // tile_cols
+    spot_masks = [
+        (lane >= spot * tile_cols) & (lane < (spot + 1) * tile_cols) for spot in range(places)
+    ]
     for row in range(rows):
         halves = []
         for half in range(block // LANES):
-            total = jnp.zeros((8, LANES), f32)
-            reach = min(cols, LANES) // tile_cols
-            turned = [
-                rolled(stacks[half * reach + j], (j - row) * tile_cols) for j in range(reach)
-            ]
-            for j, one in enumerate(turned):
-                lead = j * tile_cols
-                total = jnp.where((lane >= lead) & (lane < lead + tile_cols), one, total)
+            total = stacks[half * reach]
+            for j in range(1, reach):
+                total = jnp.where(
+                    spot_masks[(row + j) % places], stacks[half * reach + j], total
+                )
             halves.append(total)
-        across.append(jnp.concatenate(halves, axis=1))
-    spreads = 0.15 * jnp.tanh(jnp.concatenate(across, axis=0))
-    moved = [spreads] + [rolled(spreads, cols * s) for s in range(1, slots)]
-    for row in range(rows):
+        moved = []
+        for s in range(slots):
+            turned = [rolled(x, cols * s - row * tile_cols) for x in halves]
+            moved.append(turned[0] if len(turned) == 1 else jnp.concatenate(turned, axis=1))
         for source in range(3):
             at = row + DEPTH + rows * (source - 1)
             if at < 0 or at >= tall:
                 continue
             k, s = at % n, at // n
             for c in range(2):
-                line = 8 * row + 2 * source + c
+                line = 2 * source + c
                 drift[c, k : k + 1, cols * s : cols * (s + 1)] = moved[s][
                     line : line + 1, cols * s : cols * (s + 1)
                 ]
@@ -623,7 +637,7 @@
             faces2[g, planes + m : planes + m + 1, :] = 0.5 * (here + rolled(here, -1))
         return carry
 
-    lax.fori_loop(0, freqs, face_step, 0)
+    [face_step(g, 0) for g in range(freqs)]
 
     for part in range(len(PARTS)):
         await_bytes(arrive.at[rest, part_rows(part)], out_sems.at[1, part])
@@ -686,7 +700,8 @@
         return copy(back.at[f], final.at[me], back_sems, (), (), band, f)
 
     others(lambda f: back_copy(f).start())
-    final[me] = back[me]
+    keep = pltpu.make_async_copy(back.at[me], final.at[me], store_sems.at[0])
+    keep.start()
 
     stokes = jnp.dot(
         weight[...], arrive[...].reshape(total_rows, planes * LANES),
@@ -734,11 +749,8 @@
             ],
         )
     for c, field in enumerate((u, v)):
-        turned = pack(field, moves, tile_cols).T
-        for row in range(rows):
-            spot = spot_of[row]
-            vout[c, row] = turned[spot * tile_cols : (spot + 1) * tile_cols, :]
-    store_ocean = pltpu.make_async_copy(vout, ocean_out, store_sems.at[1])
+        flat[c * LAYERS : (c + 1) * LAYERS, :] = pack(field, moves, tile_cols)
+    store_ocean = pltpu.make_async_copy(flat, ocean_out, store_sems.at[1])
     store_ocean.start()
 
     await_bytes(route_out.at[rest], route_sems.at[0, 0])
@@ -758,24 +770,37 @@
         await_bytes(leave.at[rest, part_rows(part)], out_sems.at[0, part])
 
     await_bytes(final.at[rest], back_sems.at[1])
+    await_bytes(back.at[rest], back_sems.at[0])
+    store_ocean.wait()
+    keep.wait()
+
+
+def finish(final, flat, result, ocean_out):
+    freqs = final.shape[0]
+    rows, cols = result.shape[1:]
+    tile_cols = ocean_out.shape[2]
+    pitch = tile_cols + 2 * HALO
+    planes = (rows + 2 * HALO) * pitch // LANES
+    _, spot_of = packing(rows, planes, pitch, tile_cols)
     width = min(freqs, LANES // tile_cols)
     reach = width * tile_cols
     row_at = {spot: row for row, spot in spot_of.items()}
+    for c in range(2):
+        turned = flat[c * LAYERS : (c + 1) * LAYERS, :].T
+        for row in range(rows):
+            spot = spot_of[row]
+            ocean_out[c, row] = turned[spot * tile_cols : (spot + 1) * tile_cols, :]
     for chunk in range(freqs // width):
         columns = [final[chunk * width + j] for j in range(width)]
         for i, one in enumerate(swap_pieces(columns, tile_cols, width)):
             for s in range(LANES // reach):
                 row = row_at[s * width + i]
-                cells = rolled(one, -s * reach)[:, :reach]
+                cells = pltpu.roll(one, LANES - s * reach, 1) if s else one
+                cells = cells[:DIR, :reach]
                 if cols > LANES:
-                    done[:, row, chunk * reach : (chunk + 1) * reach] = cells
+                    result[:, row, chunk * reach : (chunk + 1) * reach] = cells
                 else:
-                    done.reshape(DIRP * rows, cols)[pl.ds(row, DIRP, stride=rows), :] = cells
-    store = pltpu.make_async_copy(done.at[pl.ds(0, DIR)], result, store_sems.at[0])
-    store.start()
-    await_bytes(back.at[rest], back_sems.at[0])
-    store_ocean.wait()
-    store.wait()
+                    result.reshape(DIR * rows, cols)[pl.ds(row, DIR, stride=rows), :] = cells
 
 
 def body(
@@ -803,7 +828,7 @@
     assert pitch == 2 * tile_cols and LANES % pitch == 0 and freqs * tile_cols == cols
     assert (rows + 2 * HALO) % (LANES // pitch) == 0 and cols & (cols - 1) == 0
     assert block % cols == 0 and n * block == tall * cols and cols % pitch == 0
-    assert bands > 1 and freqs > 1 and CYCLES * SUB == 8 and 2 * planes <= 8 and block // cols <= 2
+    assert bands > 1 and freqs % 4 == 0 and CYCLES * SUB == 8 and 2 * planes <= 8 and block // cols <= 2
     angles = (np.arange(DIR) + 0.5) * (2.0 * np.pi / DIR)
     waves = np.stack([np.cos(angles), np.sin(angles)])
     wave = np.zeros((DIRP, 2), np.float32)
@@ -817,20 +842,21 @@
     widen[index // DIR * DIRP + index % DIR, index] = 1.0
     f32, bf16 = jnp.float32, jnp.bfloat16
     anywhere = pl.BlockSpec(memory_space=pl.ANY)
-    scalars = pl.BlockSpec(memory_space=pltpu.SMEM)
     dma = pltpu.SemaphoreType.DMA
     vmem = pltpu.VMEM
     tile_cells = rows * tile_cols
     layers = 2 * LAYERS
-    result, ocean = pl.pallas_call(
+    final, flat = pl.pallas_call(
         functools.partial(kernel, bands, freqs, cols),
         out_shape=(
-            jax.ShapeDtypeStruct((DIR, rows, cols), f32),
-            jax.ShapeDtypeStruct((2, rows, tile_cols, LAYERS), f32),
+            jax.ShapeDtypeStruct((freqs, DIRP, LANES), f32),
+            jax.ShapeDtypeStruct((layers, LANES), f32),
         ),
-        in_specs=[scalars] * 2 + [anywhere] * 9,
+        in_specs=[anywhere] * 11,
         out_specs=(anywhere, anywhere),
         scratch_shapes=[
+            pltpu.SMEM((freqs,), jnp.int32),
+            pltpu.SMEM(stokes_route.shape[::-1], jnp.int32),
             vmem((DIRP, rows, cols), f32),
             vmem((DIRP, DEPTH, cols), f32),
             vmem((DIRP, DEPTH, cols), f32),
@@ -852,6 +878,7 @@
             vmem((SUB, planes, DIRP, LANES), f32),
             vmem((planes, DIRP, LANES), f32),
             vmem((layers, tile_cells), f32),
+            vmem((layers, tile_cells), f32),
             vmem((9, layers, tile_cells), f32),
             vmem((freqs, 2, tile_cells), f32),
             vmem((freqs, 2, tile_cells), f32),
@@ -867,12 +894,10 @@
             vmem((freqs, DIRP, planes * LANES), f32),
             vmem((freqs, DIRP, LANES), f32),
             vmem((freqs, DIRP, LANES), f32),
-            vmem((freqs, DIRP, LANES), f32),
-            vmem((DIRP, rows, cols), f32),
             vmem((layers, planes * LANES), f32),
             vmem((layers, parts), f32),
-            vmem((2, rows, tile_cols, LAYERS), f32),
-            dma((9,)),
+            vmem((layers, LANES), f32),
+            dma((11,)),
             dma((2, 2)),
             dma((2, 3)),
             dma((2,)),
@@ -896,6 +921,16 @@
         jnp.asarray(wave),
         jnp.asarray(trig.reshape(2, parts)),
     )
+    whole = pl.BlockSpec(memory_space=vmem)
+    result, ocean = pl.pallas_call(
+        finish,
+        out_shape=(
+            jax.ShapeDtypeStruct((DIR, rows, cols), f32),
+            jax.ShapeDtypeStruct((2, rows, tile_cols, LAYERS), f32),
+        ),
+        in_specs=[whole] * 2,
+        out_specs=(whole, whole),
+    )(final, flat)
     return (result.reshape(1, DIR, rows, cols), ocean.transpose(0, 3, 1, 2))
 
 

time: 37.5 us -> 36.4 us (0.971)
  local copies, waits for them, and re-layouts: 2.39 us -> 0 us
  Pallas kernels: 34.3 us -> 35.6 us
    unnamed x4 -> x0, local copies, waits for them, and re-layouts: 2.39 us -> none
    pallas_call x0 -> x1, Pallas kernels: none -> 2.05 us  [body(): pl.pallas_call(finish, out_shape=(jax.ShapeDtypeStruct((DIR, rows, cols),...]
    pallas_call x1, Pallas kernels: 34.3 us -> 33.6 us  [body(): pl.pallas_call(functools.partial(kernel, bands, freqs, cols), out_shape=(...]
where the time goes in v2:
time: 36.4 us; the launch traced here: 36.3 us
  Pallas kernels  35.6 us (98%)
  between operations  0.64 us (2%)
    pallas_call x1, Pallas kernels, body(): pl.pallas_call(functools.partial(kernel, bands, freqs, cols), out_shape=(...  33.6 us
    pallas_call x1, Pallas kernels, body(): pl.pallas_call(finish, out_shape=(jax.ShapeDtypeStruct((DIR, rows, cols),...  2.05 us

profile of v2, /device:TPU:0, one launch (start us, length us, event | category | flops | bytes accessed | tf_op | source)
XLA Modules:
  0.0 36.3 jit_solution(7526261937722775679)
XLA Ops:
  0.6 33.6 %shard_map.122 = (f32[8,40,128]{2,1,0:T(8,128)}, f32[48,128]{1,0:T(8,128)}) custom-call(s32[8]{0:T(128)} %route_in.1, s32[4,8]{1,0:T(4,128)} %bitcast.7, f32[36,16,64]{2,1,0:T(8,128)} %bitcast.5, f32[2,16,8,24]{3,2,1,0:T(8,128)} %bitcast.6, bf16[288,288]{1,0:T(8,128)(2,1)} %gain_in.1, bf16[288,288]{1,0:T(8,128)(2,1)} %quad_in.1, s32[8,64,64]{2,1,0:T(8,128)} %flags_in.1, ...), custom_call_target="tpu_custom_call" | custom-call | tf_op jit(solution)/shard_map/pallas_call | solution.py:849
  34.2 2.1 %shard_map.123 = (f32[36,16,64]{2,1,0:T(8,128)}, f32[2,16,8,24]{3,2,1,0:T(8,128)}) custom-call(f32[8,40,128]{2,1,0:T(8,128)} %get-tuple-element.6.final, f32[48,128]{1,0:T(8,128)} %get-tuple-element.7.flat), custom_call_target="tpu_custom_call" | custom-call | tf_op jit(solution)/shard_map/pallas_call | solution.py:925

commit v3 on v2

--- a/solution.py
+++ b/solution.py
@@ -29,7 +29,10 @@
 GROUPS = DIRP // GROUP
 HALO = SUB
 DEPTH = CYCLES * SUB
-PARTS = ((0, 1), (1, 3), (3, GROUPS))
+PARTS = ((0, 1), (1, 3))
+REST = 3
+QUAD = 4
+QUADS = (DIR - REST * GROUP) // QUAD
 MESH = pl.DeviceIdType.MESH
 
 
@@ -149,8 +152,14 @@
     faces2,
     coef,
     coef2,
+    start,
     leave,
+    leave_end,
+    leave_last,
     arrive,
+    arrive_end,
+    arrive_last,
+    clean,
     first,
     packed,
     back,
@@ -212,6 +221,12 @@
         shift %= x.shape[1]
         return pltpu.roll(x, shift, 1) if shift else x
 
+    def locate(at):
+        return (at, 0) if at < n else (tall - 1 - at, 1)
+
+    def row_at(k, s):
+        return tall - 1 - k if s else k
+
     def strided(ref, size, base, at):
         depth = ref.shape[1]
         if cols > LANES:
@@ -382,14 +397,17 @@
         return flag, sea
 
     for k in range(n):
-        pieces = [grid_row(k + n * s) for s in range(slots)]
+        pieces = [grid_row(row_at(k, s)) for s in range(slots)]
         flag_blk[k] = jnp.concatenate([flag for flag, _ in pieces], axis=1)
         sea = jnp.concatenate([sea for _, sea in pieces], axis=1)
         sea_blk[8 * k : 8 * (k + 1), :] = jnp.broadcast_to(sea, wide)
 
+    first_slot = lax.broadcasted_iota(jnp.int32, wide, 1) < cols
     for k in range(n):
         here = flag_blk[k]
-        above = flag_blk[k + 1] if k + 1 < n else rolled(flag_blk[0], -cols)
+        above = flag_blk[k + 1] if k + 1 < n else rolled(here, cols)
+        if slots > 1:
+            above = jnp.where(first_slot, above, here)
         beside = rolled(here, -1)
         for sub in range(SUB):
             there = slice(8 * k, 8 * (k + 1))
@@ -403,8 +421,7 @@
     for m in range(planes):
         total_flags, total_sea = jnp.zeros((8, LANES), f32), jnp.zeros((8, LANES), f32)
         for q in range(per):
-            at = m + planes * q + DEPTH - HALO
-            k, s = at % n, at // n
+            k, s = locate(m + planes * q + DEPTH - HALO)
             shift = lax.rem(q * pitch - cols * s - tile_cols * me + HALO + 2 * block, block)
             hit = (lane >= q * pitch) & (lane < (q + 1) * pitch) & inside
             total_flags = jnp.where(
@@ -445,6 +462,32 @@
         deposits = jnp.where(own, deposit, deposits)
     for c in range(2):
         weight[c * LAYERS : (c + 1) * LAYERS, :] = deposits * trig[c : c + 1, :]
+
+    @pl.when(has_low)
+    def _():
+        halo_to_high.wait_recv()
+
+    @pl.when(has_high)
+    def _():
+        halo_to_low.wait_recv()
+
+    number = me.astype(f32) + 0.5
+    my_rate = 0.5 + 0.3 * number / freqs
+
+    def row_of(base, at):
+        if at < DEPTH:
+            return strided(halo_low, GROUP, base, at)
+        if at < DEPTH + rows:
+            return strided(spec, GROUP, base, at - DEPTH)
+        return strided(halo_high, GROUP, base, at - DEPTH - rows)
+
+    starts = [
+        jnp.concatenate([row_of(group * GROUP, row_at(k, s)) for s in range(slots)], axis=1)
+        for group in range(GROUPS)
+        for k in range(n)
+    ]
+    for i, one in enumerate(starts):
+        start[i // n, 8 * (i % n) : 8 * (i % n + 1), :] = one
 
     await_bytes(route_own.at[rest], route_sems.at[1, 0])
 
@@ -484,7 +527,7 @@
             at = row + DEPTH + rows * (source - 1)
             if at < 0 or at >= tall:
                 continue
-            k, s = at % n, at // n
+            k, s = locate(at)
             for c in range(2):
                 line = 2 * source + c
                 drift[c, k : k + 1, cols * s : cols * (s + 1)] = moved[s][
@@ -494,40 +537,16 @@
     last = ((blane & (cols - 1)) == cols - 1).astype(f32)
     inner = 1.0 - last
     east, north = drift[0], drift[1]
-    above = jnp.concatenate([north[1:], rolled(north[0:1], -cols)], axis=0)
+    above = jnp.concatenate([north[1:], rolled(north[n - 1 :], cols)], axis=0)
+    sign = jnp.where(blane < cols, 1.0, -1.0)
     for i, face in enumerate(
-        (0.5 * (north + above), 0.5 * (inner * east + rolled(east, -1)), 0.5 * east)
+        (sign * (0.5 * (north + above)), 0.5 * (inner * east + rolled(east, -1)), 0.5 * east)
     ):
         for k in range(n):
             faces[i, 8 * k : 8 * (k + 1), :] = jnp.broadcast_to(face[k : k + 1], wide)
 
-    @pl.when(has_low)
-    def _():
-        halo_to_high.wait_recv()
-
-    @pl.when(has_high)
-    def _():
-        halo_to_low.wait_recv()
-
-    number = me.astype(f32) + 0.5
-    my_rate = 0.5 + 0.3 * number / freqs
-
-    def row_of(base, at):
-        if at < DEPTH:
-            return strided(halo_low, GROUP, base, at)
-        if at < DEPTH + rows:
-            return strided(spec, GROUP, base, at - DEPTH)
-        return strided(halo_high, GROUP, base, at - DEPTH - rows)
-
-    def up(x, by):
-        return jnp.concatenate([x[8:], rolled(x[:8], -by)], axis=0)
-
-    def down(x, by):
-        return jnp.concatenate([rolled(x[-8:], by), x[:-8]], axis=0)
-
-    def advect_first(group, carry):
-        base = group * GROUP
-        table = wave[pl.ds(base, GROUP), :]
+    def advect_first(group):
+        table = wave[group * GROUP : (group + 1) * GROUP, :]
 
         def rate_of(i):
             rate = jnp.broadcast_to(table[:, i : i + 1] * my_rate, wide)
@@ -535,23 +554,27 @@
 
         rate_east = rate_of(0)
         for axis, rate in ((0, rate_of(1)), (1, rate_east)):
+            if axis == 0 and slots > 1:
+                rate = rate * sign
             for i, one in enumerate(parts_of(rate + faces[axis])):
-                coef[3 * axis + i] = one
-        coef[6] = 1.0 - last * jnp.maximum(rate_east + faces[2], 0.0)
-        state = jnp.concatenate(
-            [
-                jnp.concatenate([row_of(base, k + n * s) for s in range(slots)], axis=1)
-                for k in range(n)
-            ],
-            axis=0,
-        )
+                coef[group, 3 * axis + i] = one
+        coef[group, 6] = 1.0 - last * jnp.maximum(rate_east + faces[2], 0.0)
+        state = start[group]
         for sub in range(SUB):
-            more = flag_north[sub] * coef[2]
-            flux = (coef[0] + more) * state + (coef[1] - more) * up(state, cols)
-            state = state - (flux - down(flux, cols))
-            more = flag_east[sub] * coef[5]
-            flux = (coef[3] + more) * (inner * state) + (coef[4] - more) * rolled(state, -1)
-            state = (coef[6] * state - (inner * flux - rolled(flux, 1))) * sea_blk[...]
+            here, new = slice(8 * sub, 8 * n), slice(8 * (sub + 1), 8 * n)
+            beyond = rolled(state[-8:], cols)
+            more = flag_north[sub, here] * coef[group, 2, here]
+            flux = (coef[group, 0, here] + more) * state + (
+                coef[group, 1, here] - more
+            ) * jnp.concatenate([state[8:], beyond], axis=0)
+            state = state[8:] - (flux[8:] - flux[:-8])
+            more = flag_east[sub, new] * coef[group, 5, new]
+            flux = (coef[group, 3, new] + more) * (inner * state) + (
+                coef[group, 4, new] - more
+            ) * rolled(state, -1)
+            state = (
+                coef[group, 6, new] * state - (inner * flux - rolled(flux, 1))
+            ) * sea_blk[new, :]
         width = min(cols, LANES) // pitch
         low_half = lax.broadcasted_iota(jnp.int32, (8 * planes, LANES), 1) < width * pitch
         for odd in range(2):
@@ -563,9 +586,9 @@
                     for s in range(slots):
                         lines = []
                         for m in range(planes):
-                            at = m + planes * (i + width * s) + DEPTH - HALO
-                            assert at // n == s
-                            k = at % n
+                            k, slot = locate(m + planes * (i + width * s) + DEPTH - HALO)
+                            assert slot == s and k >= SUB
+                            k -= SUB
                             lines.append(
                                 turned[8 * k : 8 * (k + 1), half * LANES : (half + 1) * LANES]
                             )
@@ -574,10 +597,15 @@
                 for e, one in enumerate(swap_pieces(sources, pitch, width)):
                     to = 2 * (e + width * half) + odd
                     for m in range(planes):
-                        leave[to, pl.ds(base, GROUP), m * LANES : (m + 1) * LANES] = one[
-                            8 * m : 8 * (m + 1)
-                        ]
-        return carry
+                        cells = one[8 * m : 8 * (m + 1)]
+                        at = slice(m * LANES, (m + 1) * LANES)
+                        if group < REST:
+                            leave[to, group * GROUP : (group + 1) * GROUP, at] = cells
+                            continue
+                        end, at = (leave_last, slice(0, LANES)) if m == planes - 1 else (leave_end, at)
+                        first_quad = (group - REST) * GROUP // QUAD
+                        for i in range(min(GROUP // QUAD, QUADS - first_quad)):
+                            end[to, first_quad + i, :, at] = cells[i * QUAD : (i + 1) * QUAD]
 
     def part_rows(part):
         low, high = PARTS[part]
@@ -589,10 +617,28 @@
             leave.at[f, there], arrive.at[me, there], out_sems, (part,), (part,), band, f
         )
 
+    ends = ((leave_end, arrive_end, len(PARTS)), (leave_last, arrive_last, len(PARTS) + 1))
+
+    def end_copy(leaving, arriving, part, f):
+        return copy(leaving.at[f], arriving.at[me], out_sems, (part,), (part,), band, f)
+
+    def received():
+        for part in range(len(PARTS)):
+            yield arrive.at[rest, part_rows(part)], part
+        for _, arriving, part in ends:
+            yield arriving.at[rest], part
+
     for part, (low, high) in enumerate(PARTS):
-        [advect_first(i, 0) for i in range(low, high)]
+        for group in range(low, high):
+            advect_first(group)
         others(lambda f: out_copy(part, f).start())
+    for group in range(REST, GROUPS):
+        advect_first(group)
+    for leaving, arriving, part in ends:
+        others(lambda f: end_copy(leaving, arriving, part, f).start())
     arrive[me] = leave[me]
+    arrive_end[me] = leave_end[me]
+    arrive_last[me] = leave_last[me]
 
     deep = 1 + has_low.astype(jnp.int32) + has_high.astype(jnp.int32)
     broad = 1 + (me > 0).astype(jnp.int32) + (me < freqs - 1).astype(jnp.int32)
@@ -639,9 +685,6 @@
 
     [face_step(g, 0) for g in range(freqs)]
 
-    for part in range(len(PARTS)):
-        await_bytes(arrive.at[rest, part_rows(part)], out_sems.at[1, part])
-
     def source(whole):
         grown = jnp.dot(gain[...], whole.astype(jnp.bfloat16), preferred_element_type=f32)
         quartic = jnp.dot(
@@ -650,13 +693,27 @@
         return whole * (1.0 + 0.5 * jnp.tanh(grown) - 0.25 * jnp.tanh(quartic))
 
     total_rows = freqs * DIRP
+    incoming = list(received())
+    for ref, part in incoming[:-1]:
+        await_bytes(ref, out_sems.at[1, part])
+    pad = jnp.zeros((DIRP - DIR, LANES), f32)
     for m in range(planes):
         there = slice(m * LANES, (m + 1) * LANES)
-        whole = arrive[:, :, there].reshape(total_rows, LANES) * sea2[m][0:1]
+        end, at = (arrive_end, there)
+        if m == planes - 1:
+            await_bytes(incoming[-1][0], out_sems.at[1, incoming[-1][1]])
+            end, at = (arrive_last, slice(0, LANES))
+        pieces = []
+        for f in range(freqs):
+            pieces.append(arrive[f, :, there])
+            pieces += [end[f, i, :, at] for i in range(QUADS)]
+            pieces.append(pad)
+        whole = jnp.concatenate(pieces, axis=0) * sea2[m][0:1]
+        clean[:, there] = whole
         first[:, :, there] = source(whole).reshape(freqs, DIRP, LANES)
 
-    def advect_second(g, carry):
-        rate = 0.5 + 0.3 * (g.astype(f32) + 0.5) / freqs
+    def advect_second(g):
+        rate = 0.5 + 0.3 * (g + 0.5) / freqs
         table = wave[...] * rate
         rate_east = jnp.broadcast_to(table[:, 0:1], (DIRP, LANES))
         rate_north = jnp.broadcast_to(table[:, 1:2], (DIRP, LANES))
@@ -665,15 +722,15 @@
             for axis, rate in ((0, rate_north), (planes, rate_east)):
                 face = faces2[g, axis + m : axis + m + 1, :]
                 for i, one in enumerate(parts_of(rate + face)):
-                    coef2[3 * (axis + m) + i] = one
+                    coef2[g, 3 * (axis + m) + i] = one
         for sub in range(SUB):
             fluxes = []
             for m in range(planes):
                 here = 3 * m
-                more = flag_north2[sub, m] * coef2[here + 2]
+                more = flag_north2[sub, m] * coef2[g, here + 2]
                 above = state[m + 1] if m + 1 < planes else rolled(state[0], -pitch)
                 fluxes.append(
-                    (coef2[here] + more) * state[m] + (coef2[here + 1] - more) * above
+                    (coef2[g, here] + more) * state[m] + (coef2[g, here + 1] - more) * above
                 )
             cells = [
                 state[m] - (fluxes[m] - (fluxes[m - 1] if m else rolled(fluxes[-1], pitch)))
@@ -682,18 +739,18 @@
             fluxes = []
             for m in range(planes):
                 here = 3 * (planes + m)
-                more = flag_east2[sub, m] * coef2[here + 2]
+                more = flag_east2[sub, m] * coef2[g, here + 2]
                 fluxes.append(
-                    (coef2[here] + more) * cells[m]
-                    + (coef2[here + 1] - more) * rolled(cells[m], -1)
+                    (coef2[g, here] + more) * cells[m]
+                    + (coef2[g, here + 1] - more) * rolled(cells[m], -1)
                 )
             state = [
                 (cells[m] - (fluxes[m] - rolled(fluxes[m], 1))) * sea2[m] for m in range(planes)
             ]
         packed[g] = pack(state, moves, tile_cols)
-        return carry
-
-    [advect_second(jnp.int32(g), 0) for g in range(freqs)]
+
+    for g in range(freqs):
+        advect_second(g)
     back[...] = source(packed[...].reshape(total_rows, LANES)).reshape(freqs, DIRP, LANES)
 
     def back_copy(f):
@@ -704,7 +761,7 @@
     keep.start()
 
     stokes = jnp.dot(
-        weight[...], arrive[...].reshape(total_rows, planes * LANES),
+        weight[...], clean[...],
         precision=precise, preferred_element_type=f32,
     )
     level = lax.broadcasted_iota(jnp.int32, (LAYERS, LANES), 0)
@@ -768,6 +825,8 @@
     await_tiles(0)
     for part in range(len(PARTS)):
         await_bytes(leave.at[rest, part_rows(part)], out_sems.at[0, part])
+    for leaving, _, part in ends:
+        await_bytes(leaving.at[rest], out_sems.at[0, part])
 
     await_bytes(final.at[rest], back_sems.at[1])
     await_bytes(back.at[rest], back_sems.at[0])
@@ -827,7 +886,7 @@
     assert rows * tile_cols == LANES and rows >= DEPTH and tile_cols >= HALO >= OSTEPS
     assert pitch == 2 * tile_cols and LANES % pitch == 0 and freqs * tile_cols == cols
     assert (rows + 2 * HALO) % (LANES // pitch) == 0 and cols & (cols - 1) == 0
-    assert block % cols == 0 and n * block == tall * cols and cols % pitch == 0
+    assert block % cols == 0 and rows % 2 == 0 and n * block == tall * cols and cols % pitch == 0
     assert bands > 1 and freqs % 4 == 0 and CYCLES * SUB == 8 and 2 * planes <= 8 and block // cols <= 2
     angles = (np.arange(DIR) + 0.5) * (2.0 * np.pi / DIR)
     waves = np.stack([np.cos(angles), np.sin(angles)])
@@ -846,6 +905,11 @@
     vmem = pltpu.VMEM
     tile_cells = rows * tile_cols
     layers = 2 * LAYERS
+    leaving = [
+        vmem((freqs, REST * GROUP, planes * LANES), f32),
+        vmem((freqs, QUADS, QUAD, (planes - 1) * LANES), f32),
+        vmem((freqs, QUADS, QUAD, LANES), f32),
+    ]
     final, flat = pl.pallas_call(
         functools.partial(kernel, bands, freqs, cols),
         out_shape=(
@@ -887,10 +951,12 @@
             vmem((2, n, block), f32),
             vmem((3, 8 * n, block), f32),
             vmem((freqs, 8, LANES), f32),
-            vmem((7, 8 * n, block), f32),
-            vmem((6 * planes, DIRP, LANES), f32),
-            vmem((freqs, DIRP, planes * LANES), f32),
-            vmem((freqs, DIRP, planes * LANES), f32),
+            vmem((GROUPS, 7, 8 * n, block), f32),
+            vmem((freqs, 6 * planes, DIRP, LANES), f32),
+            vmem((GROUPS, 8 * n, block), f32),
+            *leaving,
+            *leaving,
+            vmem((parts, planes * LANES), f32),
             vmem((freqs, DIRP, planes * LANES), f32),
             vmem((freqs, DIRP, LANES), f32),
             vmem((freqs, DIRP, LANES), f32),
@@ -901,7 +967,7 @@
             dma((2, 2)),
             dma((2, 3)),
             dma((2,)),
-            dma((2, len(PARTS))),
+            dma((2, len(PARTS) + 2)),
             dma((2,)),
             dma((2,)),
         ],

time: 36.4 us -> 34.2 us (0.940)
  Pallas kernels: 35.6 us -> 33.4 us
    pallas_call x1, Pallas kernels: 33.6 us -> 31.4 us  [body(): pl.pallas_call(functools.partial(kernel, bands, freqs, cols), out_shape=(...]
where the time goes in v3:
time: 34.2 us; the launch traced here: 34.1 us
  Pallas kernels  33.4 us (98%)
  between operations  0.64 us (2%)
    pallas_call x1, Pallas kernels, body(): pl.pallas_call(functools.partial(kernel, bands, freqs, cols), out_shape=(...  31.4 us
    pallas_call x1, Pallas kernels, body(): pl.pallas_call(finish, out_shape=(jax.ShapeDtypeStruct((DIR, rows, cols),...  2.05 us

profile of v3, /device:TPU:0, one launch (start us, length us, event | category | flops | bytes accessed | tf_op | source)
XLA Modules:
  0.0 34.1 jit_solution(1482016406325813685)
XLA Ops:
  0.6 31.4 %shard_map.122 = (f32[8,40,128]{2,1,0:T(8,128)}, f32[48,128]{1,0:T(8,128)}) custom-call(s32[8]{0:T(128)} %route_in.1, s32[4,8]{1,0:T(4,128)} %bitcast.7, f32[36,16,64]{2,1,0:T(8,128)} %bitcast.5, f32[2,16,8,24]{3,2,1,0:T(8,128)} %bitcast.6, bf16[288,288]{1,0:T(8,128)(2,1)} %gain_in.1, bf16[288,288]{1,0:T(8,128)(2,1)} %quad_in.1, s32[8,64,64]{2,1,0:T(8,128)} %flags_in.1, ...), custom_call_target="tpu_custom_call" | custom-call | tf_op jit(solution)/shard_map/pallas_call | solution.py:913
  32.0 2.1 %shard_map.123 = (f32[36,16,64]{2,1,0:T(8,128)}, f32[2,16,8,24]{3,2,1,0:T(8,128)}) custom-call(f32[8,40,128]{2,1,0:T(8,128)} %get-tuple-element.6.final, f32[48,128]{1,0:T(8,128)} %get-tuple-element.7.flat), custom_call_target="tpu_custom_call" | custom-call | tf_op jit(solution)/shard_map/pallas_call | solution.py:991

commit v4 on v3

--- a/solution.py
+++ b/solution.py
@@ -27,6 +27,8 @@
 LANES = 128
 DIRP = -(-DIR // GROUP) * GROUP
 GROUPS = DIRP // GROUP
+FULL = DIR // GROUP * GROUP
+TAIL = DIR - FULL
 HALO = SUB
 DEPTH = CYCLES * SUB
 PARTS = ((0, 1), (1, 3))
@@ -431,13 +433,13 @@
         window_flags.append(total_flags)
         window_sea.append(total_sea)
     for m in range(planes):
-        sea2[m] = jnp.concatenate([window_sea[m]] * GROUPS, axis=0)
+        sea2[m] = jnp.concatenate([window_sea[m]] * (FULL // 8), axis=0)
         above = window_flags[m + 1] if m + 1 < planes else rolled(window_flags[0], -pitch)
         beside = rolled(window_flags[m], -1)
         for sub in range(SUB):
             step = SUB + sub
-            flag_north2[sub, m] = jnp.broadcast_to(above[step : step + 1], (DIRP, LANES))
-            flag_east2[sub, m] = jnp.broadcast_to(beside[step : step + 1], (DIRP, LANES))
+            flag_north2[sub, m] = jnp.broadcast_to(above[step : step + 1], (FULL, LANES))
+            flag_east2[sub, m] = jnp.broadcast_to(beside[step : step + 1], (FULL, LANES))
 
     load_spec.wait()
     load_stokes.wait()
@@ -451,14 +453,16 @@
         ).astype(jnp.bfloat16)
 
     layer = lax.broadcasted_iota(jnp.int32, (LAYERS, 1), 0)
-    component = lax.broadcasted_iota(jnp.int32, (LAYERS, freqs * DIRP), 1)
-    deposits = jnp.zeros((LAYERS, freqs * DIRP), f32)
+    component = lax.broadcasted_iota(jnp.int32, (LAYERS, freqs * DIR), 1)
+    deposits = jnp.zeros((LAYERS, freqs * DIR), f32)
     for g in range(freqs):
         deposit = jnp.zeros((LAYERS, 1), f32)
         for j in range(stokes_route.shape[0]):
             hit = (layer == stokes_route[j, g]).astype(f32)
             deposit = deposit + hit * (1.0 / (1.0 + j))
-        own = (component >= g * DIRP) & (component < (g + 1) * DIRP)
+        tail = freqs * FULL + g * TAIL
+        own = (component >= g * FULL) & (component < (g + 1) * FULL)
+        own = own | ((component >= tail) & (component < tail + TAIL))
         deposits = jnp.where(own, deposit, deposits)
     for c in range(2):
         weight[c * LAYERS : (c + 1) * LAYERS, :] = deposits * trig[c : c + 1, :]
@@ -466,10 +470,12 @@
     @pl.when(has_low)
     def _():
         halo_to_high.wait_recv()
+        await_bytes(route_low, route_sems.at[1, 2])
 
     @pl.when(has_high)
     def _():
         halo_to_low.wait_recv()
+        await_bytes(route_high, route_sems.at[1, 1])
 
     number = me.astype(f32) + 0.5
     my_rate = 0.5 + 0.3 * number / freqs
@@ -490,14 +496,6 @@
         start[i // n, 8 * (i % n) : 8 * (i % n + 1), :] = one
 
     await_bytes(route_own.at[rest], route_sems.at[1, 0])
-
-    @pl.when(has_low)
-    def _():
-        await_bytes(route_low, route_sems.at[1, 2])
-
-    @pl.when(has_high)
-    def _():
-        await_bytes(route_high, route_sems.at[1, 1])
 
     stacks = [
         jnp.concatenate(
@@ -692,11 +690,10 @@
         )
         return whole * (1.0 + 0.5 * jnp.tanh(grown) - 0.25 * jnp.tanh(quartic))
 
-    total_rows = freqs * DIRP
+    total_rows = freqs * DIR
     incoming = list(received())
     for ref, part in incoming[:-1]:
         await_bytes(ref, out_sems.at[1, part])
-    pad = jnp.zeros((DIRP - DIR, LANES), f32)
     for m in range(planes):
         there = slice(m * LANES, (m + 1) * LANES)
         end, at = (arrive_end, there)
@@ -706,22 +703,18 @@
         pieces = []
         for f in range(freqs):
             pieces.append(arrive[f, :, there])
-            pieces += [end[f, i, :, at] for i in range(QUADS)]
-            pieces.append(pad)
+            pieces += [end[f, i, :, at] for i in range(QUADS - 1)]
+        pieces += [end[f, QUADS - 1, :, at] for f in range(freqs)]
         whole = jnp.concatenate(pieces, axis=0) * sea2[m][0:1]
         clean[:, there] = whole
-        first[:, :, there] = source(whole).reshape(freqs, DIRP, LANES)
-
-    def advect_second(g):
-        rate = 0.5 + 0.3 * (g + 0.5) / freqs
-        table = wave[...] * rate
-        rate_east = jnp.broadcast_to(table[:, 0:1], (DIRP, LANES))
-        rate_north = jnp.broadcast_to(table[:, 1:2], (DIRP, LANES))
-        state = [first[g, :, m * LANES : (m + 1) * LANES] for m in range(planes)]
+        first[:, there] = source(whole)
+
+    def advect_second(g, at, rates, face_of):
+        rate_east, rate_north = [jnp.broadcast_to(x, (FULL, LANES)) for x in rates]
+        state = [first[at, m * LANES : (m + 1) * LANES] for m in range(planes)]
         for m in range(planes):
             for axis, rate in ((0, rate_north), (planes, rate_east)):
-                face = faces2[g, axis + m : axis + m + 1, :]
-                for i, one in enumerate(parts_of(rate + face)):
+                for i, one in enumerate(parts_of(rate + face_of(axis + m))):
                     coef2[g, 3 * (axis + m) + i] = one
         for sub in range(SUB):
             fluxes = []
@@ -747,11 +740,39 @@
             state = [
                 (cells[m] - (fluxes[m] - rolled(fluxes[m], 1))) * sea2[m] for m in range(planes)
             ]
-        packed[g] = pack(state, moves, tile_cols)
+        packed[at, :] = pack(state, moves, tile_cols)
 
     for g in range(freqs):
-        advect_second(g)
-    back[...] = source(packed[...].reshape(total_rows, LANES)).reshape(freqs, DIRP, LANES)
+        speed = 0.5 + 0.3 * (g + 0.5) / freqs
+        table = wave[:FULL, :] * speed
+        advect_second(
+            g,
+            slice(g * FULL, (g + 1) * FULL),
+            (table[:, 0:1], table[:, 1:2]),
+            lambda i: faces2[g, i : i + 1, :],
+        )
+    share = FULL // TAIL
+    for chunk in range(freqs // share):
+        table = wave[DIRP + chunk * FULL : DIRP + (chunk + 1) * FULL, :]
+        advect_second(
+            freqs + chunk,
+            slice((freqs + chunk) * FULL, (freqs + chunk + 1) * FULL),
+            (table[:, 0:1], table[:, 1:2]),
+            lambda i: jnp.concatenate(
+                [
+                    jnp.broadcast_to(faces2[chunk * share + j, i : i + 1, :], (TAIL, LANES))
+                    for j in range(share)
+                ],
+                axis=0,
+            ),
+        )
+    updated = source(packed[...])
+    for f in range(freqs):
+        for i in range(FULL // QUAD):
+            at = f * FULL + i * QUAD
+            back[f, i] = updated[at : at + QUAD]
+        at = freqs * FULL + f * TAIL
+        back[f, FULL // QUAD] = updated[at : at + TAIL]
 
     def back_copy(f):
         return copy(back.at[f], final.at[me], back_sems, (), (), band, f)
@@ -850,12 +871,17 @@
             spot = spot_of[row]
             ocean_out[c, row] = turned[spot * tile_cols : (spot + 1) * tile_cols, :]
     for chunk in range(freqs // width):
-        columns = [final[chunk * width + j] for j in range(width)]
+        columns = [
+            jnp.concatenate(
+                [final[chunk * width + j, i] for i in range(DIR // QUAD)], axis=0
+            )
+            for j in range(width)
+        ]
         for i, one in enumerate(swap_pieces(columns, tile_cols, width)):
             for s in range(LANES // reach):
                 row = row_at[s * width + i]
                 cells = pltpu.roll(one, LANES - s * reach, 1) if s else one
-                cells = cells[:DIR, :reach]
+                cells = cells[:, :reach]
                 if cols > LANES:
                     result[:, row, chunk * reach : (chunk + 1) * reach] = cells
                 else:
@@ -881,24 +907,29 @@
     tall = rows + 2 * DEPTH
     block = max(LANES, cols)
     n = tall * cols // block
-    parts = freqs * DIRP
+    parts = freqs * DIR
     assert CYCLES == 2 and spectrum.shape[0] == 1 and rows % 8 == 0 and DEPTH % 8 == 0
     assert rows * tile_cols == LANES and rows >= DEPTH and tile_cols >= HALO >= OSTEPS
     assert pitch == 2 * tile_cols and LANES % pitch == 0 and freqs * tile_cols == cols
     assert (rows + 2 * HALO) % (LANES // pitch) == 0 and cols & (cols - 1) == 0
     assert block % cols == 0 and rows % 2 == 0 and n * block == tall * cols and cols % pitch == 0
-    assert bands > 1 and freqs % 4 == 0 and CYCLES * SUB == 8 and 2 * planes <= 8 and block // cols <= 2
+    assert bands > 1 and freqs * TAIL % FULL == 0 and TAIL == QUAD and 2 * TAIL == GROUP and CYCLES * SUB == 8 and 2 * planes <= 8 and block // cols <= 2
     angles = (np.arange(DIR) + 0.5) * (2.0 * np.pi / DIR)
     waves = np.stack([np.cos(angles), np.sin(angles)])
-    wave = np.zeros((DIRP, 2), np.float32)
+    comps = freqs * DIR
+    which, dirs = np.divmod(np.arange(comps), DIR)
+    order = np.where(
+        dirs < FULL, which * FULL + dirs, freqs * FULL + which * TAIL + dirs - FULL
+    )
+    wave = np.zeros((DIRP + freqs * TAIL, 2), np.float32)
     wave[:DIR] = waves.T
+    speeds = 0.5 + 0.3 * (np.arange(freqs) + 0.5) / freqs
+    wave[DIRP:] = (speeds[:, None, None] * waves.T[FULL:]).reshape(-1, 2)
     factor = (0.5 + 1.5 * (np.arange(freqs) + 0.5) / freqs) * DIR ** (-0.5)
-    trig = np.zeros((2, freqs, DIRP), np.float32)
-    trig[:, :, :DIR] = waves[:, None, :] * factor[None, :, None]
-    comps = freqs * DIR
-    widen = np.zeros((parts, comps), np.float32)
-    index = np.arange(comps)
-    widen[index // DIR * DIRP + index % DIR, index] = 1.0
+    trig = np.zeros((2, comps), np.float32)
+    trig[:, order] = waves[:, dirs] * factor[which]
+    widen = np.zeros((comps, comps), np.float32)
+    widen[order, np.arange(comps)] = 1.0
     f32, bf16 = jnp.float32, jnp.bfloat16
     anywhere = pl.BlockSpec(memory_space=pl.ANY)
     dma = pltpu.SemaphoreType.DMA
@@ -913,7 +944,7 @@
     final, flat = pl.pallas_call(
         functools.partial(kernel, bands, freqs, cols),
         out_shape=(
-            jax.ShapeDtypeStruct((freqs, DIRP, LANES), f32),
+            jax.ShapeDtypeStruct((freqs, DIR // QUAD, QUAD, LANES), f32),
             jax.ShapeDtypeStruct((layers, LANES), f32),
         ),
         in_specs=[anywhere] * 11,
@@ -928,7 +959,7 @@
             vmem((comps, comps), bf16),
             vmem((comps, comps), bf16),
             vmem((parts, comps), bf16),
-            vmem((DIRP, 2), f32),
+            vmem(wave.shape, f32),
             vmem((2, parts), f32),
             vmem((parts, parts), bf16),
             vmem((parts, parts), bf16),
@@ -938,9 +969,9 @@
             vmem((8 * n, block), f32),
             vmem((SUB, 8 * n, block), f32),
             vmem((SUB, 8 * n, block), f32),
-            vmem((SUB, planes, DIRP, LANES), f32),
-            vmem((SUB, planes, DIRP, LANES), f32),
-            vmem((planes, DIRP, LANES), f32),
+            vmem((SUB, planes, FULL, LANES), f32),
+            vmem((SUB, planes, FULL, LANES), f32),
+            vmem((planes, FULL, LANES), f32),
             vmem((layers, tile_cells), f32),
             vmem((layers, tile_cells), f32),
             vmem((9, layers, tile_cells), f32),
@@ -952,14 +983,14 @@
             vmem((3, 8 * n, block), f32),
             vmem((freqs, 8, LANES), f32),
             vmem((GROUPS, 7, 8 * n, block), f32),
-            vmem((freqs, 6 * planes, DIRP, LANES), f32),
+            vmem((parts // FULL, 6 * planes, FULL, LANES), f32),
             vmem((GROUPS, 8 * n, block), f32),
             *leaving,
             *leaving,
             vmem((parts, planes * LANES), f32),
-            vmem((freqs, DIRP, planes * LANES), f32),
-            vmem((freqs, DIRP, LANES), f32),
-            vmem((freqs, DIRP, LANES), f32),
+            vmem((parts, planes * LANES), f32),
+            vmem((parts, LANES), f32),
+            vmem((freqs, DIR // QUAD, QUAD, LANES), f32),
             vmem((layers, planes * LANES), f32),
             vmem((layers, parts), f32),
             vmem((layers, LANES), f32),
@@ -985,7 +1016,7 @@
         sea_mask,
         jnp.asarray(widen, bf16),
         jnp.asarray(wave),
-        jnp.asarray(trig.reshape(2, parts)),
+        jnp.asarray(trig),
     )
     whole = pl.BlockSpec(memory_space=vmem)
     result, ocean = pl.pallas_call(

time: 34.2 us -> 34.1 us (level)
  no operation moved by 1% of the time
where the time goes in v4:
time: 34.1 us; the launch traced here: 34 us
  Pallas kernels  33.3 us (98%)
  between operations  0.64 us (2%)
    pallas_call x1, Pallas kernels, body(): pl.pallas_call(functools.partial(kernel, bands, freqs, cols), out_shape=(...  31.3 us
    pallas_call x1, Pallas kernels, body(): pl.pallas_call(finish, out_shape=(jax.ShapeDtypeStruct((DIR, rows, cols),...  2.07 us

profile of v4, /device:TPU:0, one launch (start us, length us, event | category | flops | bytes accessed | tf_op | source)
XLA Modules:
  0.0 34.0 jit_solution(5172177715082307897)
XLA Ops:
  0.6 31.3 %shard_map.122 = (f32[8,9,4,128]{3,2,1,0:T(4,128)}, f32[48,128]{1,0:T(8,128)}) custom-call(s32[8]{0:T(128)} %route_in.1, s32[4,8]{1,0:T(4,128)} %bitcast.7, f32[36,16,64]{2,1,0:T(8,128)} %bitcast.5, f32[2,16,8,24]{3,2,1,0:T(8,128)} %bitcast.6, bf16[288,288]{1,0:T(8,128)(2,1)} %gain_in.1, bf16[288,288]{1,0:T(8,128)(2,1)} %quad_in.1, s32[8,64,64]{2,1,0:T(8,128)} %flags_in.1, ...), custom_call_target="tpu_custom_call" | custom-call | tf_op jit(solution)/shard_map/pallas_call | solution.py:944
  31.9 2.1 %shard_map.123 = (f32[36,16,64]{2,1,0:T(8,128)}, f32[2,16,8,24]{3,2,1,0:T(8,128)}) custom-call(f32[8,9,4,128]{3,2,1,0:T(4,128)} %get-tuple-element.6.final, f32[48,128]{1,0:T(8,128)} %get-tuple-element.7.flat), custom_call_target="tpu_custom_call" | custom-call | tf_op jit(solution)/shard_map/pallas_call | solution.py:1022

commit v5 on v4

--- a/solution.py
+++ b/solution.py
@@ -201,8 +201,20 @@
     for i in range(mid):
         partners += near[i : i + 1] + [far[i]]
 
-    def others(fn):
-        for f in partners:
+    def across(mask):
+        total, bit = 0, 1
+        while bit < freqs:
+            on = lax.rem(me // bit, 2)
+            total = total + bit * (1 - on if mask & bit else on)
+            bit *= 2
+        return total
+
+    distant = [across(mask) for mask in range(freqs - 1, 0, -1)]
+    rising = [i + (i >= me).astype(jnp.int32) for i in range(freqs - 1)]
+    ring = [lax.rem(me + i, freqs) for i in range(1, freqs)]
+
+    def others(fn, order=None):
+        for f in order or partners:
             fn(f)
 
     def every(fn):
@@ -766,18 +778,34 @@
                 axis=0,
             ),
         )
-    updated = source(packed[...])
-    for f in range(freqs):
-        for i in range(FULL // QUAD):
-            at = f * FULL + i * QUAD
-            back[f, i] = updated[at : at + QUAD]
-        at = freqs * FULL + f * TAIL
-        back[f, FULL // QUAD] = updated[at : at + TAIL]
-
     def back_copy(f):
         return copy(back.at[f], final.at[me], back_sems, (), (), band, f)
 
-    others(lambda f: back_copy(f).start())
+    whole = packed[...]
+    rounded, squared = whole.astype(jnp.bfloat16), (whole * whole).astype(jnp.bfloat16)
+
+    def source_rows(low, high):
+        at = slice(low, high)
+        grown = jnp.dot(gain[at, :], rounded, preferred_element_type=f32)
+        quartic = jnp.dot(quad[at, :], squared, preferred_element_type=f32)
+        return whole[at] * (1.0 + 0.5 * jnp.tanh(grown) - 0.25 * jnp.tanh(quartic))
+
+    tails = freqs * FULL
+    early = 2
+    for low, high, tail_low, tail_high in (
+        (0, early, 0, 2 * early), (early, freqs, 2 * early, freqs),
+    ):
+        body_rows = source_rows(low * FULL, high * FULL)
+        tail_rows = source_rows(tails + tail_low * TAIL, tails + tail_high * TAIL)
+        for f in range(low, high):
+            for i in range(FULL // QUAD):
+                at = (f - low) * FULL + i * QUAD
+                back[f, i] = body_rows[at : at + QUAD]
+        for f in range(tail_low, tail_high):
+            at = (f - tail_low) * TAIL
+            back[f, FULL // QUAD] = tail_rows[at : at + TAIL]
+        for f in rising[:1] if low == 0 else rising[1:]:
+            back_copy(f).start()
     keep = pltpu.make_async_copy(back.at[me], final.at[me], store_sems.at[0])
     keep.start()
 

time: 34.1 us -> 33.1 us (0.971)
  Pallas kernels: 33.3 us -> 32.3 us
    pallas_call x1, Pallas kernels: 31.3 us -> 30.3 us  [body(): pl.pallas_call(functools.partial(kernel, bands, freqs, cols), out_shape=(...]
where the time goes in v5:
time: 33.1 us; the launch traced here: 33 us
  Pallas kernels  32.3 us (98%)
  between operations  0.64 us (2%)
    pallas_call x1, Pallas kernels, body(): pl.pallas_call(functools.partial(kernel, bands, freqs, cols), out_shape=(...  30.3 us
    pallas_call x1, Pallas kernels, body(): pl.pallas_call(finish, out_shape=(jax.ShapeDtypeStruct((DIR, rows, cols),...  2.07 us

profile of v5, /device:TPU:0, one launch (start us, length us, event | category | flops | bytes accessed | tf_op | source)
XLA Modules:
  0.0 33.0 jit_solution(17663717652950919660)
XLA Ops:
  0.6 30.3 %shard_map.122 = (f32[8,9,4,128]{3,2,1,0:T(4,128)}, f32[48,128]{1,0:T(8,128)}) custom-call(s32[8]{0:T(128)} %route_in.1, s32[4,8]{1,0:T(4,128)} %bitcast.7, f32[36,16,64]{2,1,0:T(8,128)} %bitcast.5, f32[2,16,8,24]{3,2,1,0:T(8,128)} %bitcast.6, bf16[288,288]{1,0:T(8,128)(2,1)} %gain_in.1, bf16[288,288]{1,0:T(8,128)(2,1)} %quad_in.1, s32[8,64,64]{2,1,0:T(8,128)} %flags_in.1, ...), custom_call_target="tpu_custom_call" | custom-call | tf_op jit(solution)/shard_map/pallas_call | solution.py:972
  30.9 2.1 %shard_map.123 = (f32[36,16,64]{2,1,0:T(8,128)}, f32[2,16,8,24]{3,2,1,0:T(8,128)}) custom-call(f32[8,9,4,128]{3,2,1,0:T(4,128)} %get-tuple-element.6.final, f32[48,128]{1,0:T(8,128)} %get-tuple-element.7.flat), custom_call_target="tpu_custom_call" | custom-call | tf_op jit(solution)/shard_map/pallas_call | solution.py:1050
